TPU v7x, 32 devices: a whole 2x2x4 slice. The times are simulated.
32 devices in a mesh: groups: 2 (over x), segment: 4 (over y, core), head: 4 (over z).
Axes of the slice: x: 2, y: 2, z: 4, core: 2. Of those that a mesh axis runs over, the one named last changes fastest.
Arguments:
- token_ids: int32 [6, 256], P('groups'), parts along dimension 0, may hold values from 0 to 18991, as said below
- embed_table: bfloat16 [18992, 256], P(('segment', 'head')), may hold values from -6 to 6
- arriving: bfloat16 [8, 256, 256], P(('groups', 'segment')), parts along dimension 0, may hold values from -16 to 16
- returning: bfloat16 [8, 256, 256], P(('groups', 'segment')), parts along dimension 0, may hold values from -6 to 6
- stashed: bfloat16 [8, 3, 256, 256], P(('groups', 'segment')), parts along dimension 0, may hold values from -16 to 16
- seed_grad: bfloat16 [6, 256, 256], P('groups'), parts along dimension 0, may hold values from -6 to 6
- expand: bfloat16 [4, 256, 2048], P('segment'), may hold values from -0.375 to 0.375
- compress: bfloat16 [4, 2048, 256], P('segment'), may hold values from -0.125 to 0.125
- norm_gain: float32 [4, 2048], P('segment'), may hold values from 0.1 to 1.9
- w_query: bfloat16 [4, 2048, 4096], P('segment', None, 'head'), may hold values from -0.125 to 0.125
- key_weight: bfloat16 [4, 2048, 512], P('segment'), may hold values from -0.125 to 0.125
- value_weight: bfloat16 [4, 2048, 512], P('segment'), may hold values from -0.125 to 0.125
- w_out: bfloat16 [4, 4096, 2048], P('segment', 'head'), may hold values from -0.09375 to 0.09375
Outputs:
- sent_forward: bfloat16 [8, 3, 256, 256], P(('groups', 'segment'), None, 'head'), parts along dimension 0
- sent_backward: bfloat16 [8, 3, 256, 256], P(('groups', 'segment'), None, 'head'), parts along dimension 0
There are 2 independent parts, one for each index of `groups`. A program takes and returns all parts, laid end to end along the dimension named above; an argument that names none is the same for every part. Nothing has to cross between parts.
Inputs may be any that keep to these rules, and one draw needn't show every extreme that they name: `token_ids`: every aligned block of 1187 ids is named by some token.
All inputs are finite; a program needn't handle non-finite values.
Results may differ from a plain program's by a relative error of at most 0.02.
Values may be sent and summed in bfloat16 or wider, within the bound.
A program may use at most 128 MiB of HBM per device.

v0:
```python
import math
import jax
import jax.numpy as jnp
from jax import lax
from jax.sharding import PartitionSpec as P

QUERY_HEADS = 32
KEY_VALUE_HEADS = 4
HEAD_SIZE = 128
EPS = 1e-06


def passed_along(x, axis, by):
    length = lax.axis_size(axis)
    pairs = [(i, i + by) for i in range(length) if 0 <= i + by < length]
    return lax.ppermute(x, axis, pairs)


def rms_scale(matrix):
    return lax.rsqrt(jnp.mean(matrix * matrix, axis=-1, keepdims=True) + EPS)


def precise(former, latter):
    return jnp.dot(
        former, latter, precision=lax.Precision.HIGHEST, preferred_element_type=jnp.float32
    )


def precise_back(former, latter):
    return lax.dot_general(
        former,
        latter,
        (((1,), (1,)), ((), ())),
        precision=lax.Precision.HIGHEST,
        preferred_element_type=jnp.float32,
    )


def narrow_back(former, latter):
    return lax.dot_general(
        former, latter, (((1,), (1,)), ((), ())), preferred_element_type=jnp.float32
    )


def norm_back(upstream_in, grad_hat):
    scaling = rms_scale(upstream_in)
    return scaling * grad_hat - upstream_in * scaling**3 * jnp.mean(
        grad_hat * upstream_in, axis=-1, keepdims=True
    )


def section_inputs(coeffs, expand_here, gain_here, query_here, key_here, value_here):
    row_count = coeffs.shape[0]
    hidden = jnp.dot(coeffs, expand_here, preferred_element_type=jnp.float32)
    scaling = rms_scale(hidden)
    normed = (hidden * scaling * gain_here).astype(jnp.bfloat16)
    queries = jnp.dot(normed, query_here, preferred_element_type=jnp.float32).reshape(
        row_count, -1, HEAD_SIZE
    )
    key_rows = jnp.dot(normed, key_here, preferred_element_type=jnp.float32).reshape(
        row_count, -1, HEAD_SIZE
    )
    values = (
        jnp.dot(normed, value_here, preferred_element_type=jnp.float32)
        .astype(jnp.bfloat16)
        .reshape(row_count, -1, HEAD_SIZE)
    )
    q_hat = (queries * rms_scale(queries)).astype(jnp.bfloat16)
    k_hat = (key_rows * rms_scale(key_rows)).astype(jnp.bfloat16)
    return (hidden, scaling, queries, key_rows, q_hat, k_hat, values)


def probabilities(q_hat, k_hat):
    row_count, head_count, head_width = q_hat.shape
    kv_heads = k_hat.shape[1]
    grouped = q_hat.reshape(row_count, kv_heads, head_count // kv_heads, head_width)
    scores = jnp.einsum(
        "iknd,jkd->knij", grouped, k_hat, preferred_element_type=jnp.float32
    ) / math.sqrt(head_width)
    causal = jnp.arange(row_count)[None, :] <= jnp.arange(row_count)[:, None]
    weights = jnp.where(causal, jnp.exp(scores), 0.0)
    return weights / jnp.sum(weights, axis=-1, keepdims=True)


def section_forward(coeffs, expand_here, gain_here, query_here, key_here, value_here, out_folded):
    hidden, scaling, queries, key_rows, q_hat, k_hat, values = section_inputs(
        coeffs, expand_here, gain_here, query_here, key_here, value_here
    )
    weights = probabilities(q_hat, k_hat)
    attended = jnp.einsum(
        "knij,jkd->iknd", weights.astype(jnp.bfloat16), values, preferred_element_type=jnp.float32
    )
    attended = attended.reshape(coeffs.shape[0], -1).astype(jnp.bfloat16)
    return jnp.dot(attended, out_folded, preferred_element_type=jnp.float32)


def section_backward(
    coeffs, grads, expand_here, gain_here, query_here, key_here, value_here, out_folded
):
    row_count = coeffs.shape[0]
    hidden, scaling, queries, key_rows, q_hat, k_hat, values = section_inputs(
        coeffs, expand_here, gain_here, query_here, key_here, value_here
    )
    weights = probabilities(q_hat, k_hat)
    head_count = queries.shape[1]
    kv_heads = key_rows.shape[1]
    query_group_size = head_count // kv_heads
    grad_attended = narrow_back(grads, out_folded).astype(jnp.bfloat16)
    grad_attended = grad_attended.reshape(row_count, kv_heads, query_group_size, HEAD_SIZE)
    grad_weights = jnp.einsum(
        "iknd,jkd->knij", grad_attended, values, preferred_element_type=jnp.float32
    )
    grad_scores = (
        weights
        * (grad_weights - jnp.sum(grad_weights * weights, axis=-1, keepdims=True))
        / math.sqrt(HEAD_SIZE)
    )
    grad_scores = grad_scores.astype(jnp.bfloat16)
    grouped = q_hat.reshape(row_count, kv_heads, query_group_size, HEAD_SIZE)
    grad_qhat = jnp.einsum(
        "knij,jkd->iknd", grad_scores, k_hat, preferred_element_type=jnp.float32
    ).reshape(row_count, head_count, HEAD_SIZE)
    grad_khat = jnp.einsum(
        "knij,iknd->jkd", grad_scores, grouped, preferred_element_type=jnp.float32
    )
    grad_values = jnp.einsum(
        "knij,iknd->jkd",
        weights.astype(jnp.bfloat16),
        grad_attended,
        preferred_element_type=jnp.float32,
    )
    grad_values = grad_values.reshape(row_count, -1).astype(jnp.bfloat16)
    grad_queries = norm_back(queries, grad_qhat).reshape(row_count, -1).astype(jnp.bfloat16)
    grad_keys = norm_back(key_rows, grad_khat).reshape(row_count, -1).astype(jnp.bfloat16)
    grad_normed = (
        narrow_back(grad_queries, query_here)
        + narrow_back(grad_keys, key_here)
        + narrow_back(grad_values, value_here)
    )
    weighted = grad_normed * gain_here
    grad_hidden = scaling * weighted - hidden * scaling**3 * jnp.mean(
        weighted * hidden, axis=-1, keepdims=True
    )
    return narrow_back(grad_hidden.astype(jnp.bfloat16), expand_here)


def shards(
    token_ids,
    embed_table,
    arriving,
    returning,
    stashed,
    seed_grad,
    expand,
    compress,
    norm_gain,
    w_query,
    key_weight,
    value_weight,
    w_out,
):
    segment_index = lax.axis_index("segment")
    last_segment = lax.axis_size("segment") - 1
    head_index = lax.axis_index("head")
    heads_here = w_query.shape[2] // HEAD_SIZE
    query_group_size = QUERY_HEADS // KEY_VALUE_HEADS
    kv_here = (heads_here + query_group_size - 1) // query_group_size
    first_kv = head_index * heads_here // query_group_size
    expand_here = expand[0]
    gain_here = norm_gain[0]
    query_here = w_query[0]
    key_here = lax.dynamic_slice_in_dim(key_weight[0], first_kv * HEAD_SIZE, kv_here * HEAD_SIZE, 1)
    value_here = lax.dynamic_slice_in_dim(
        value_weight[0], first_kv * HEAD_SIZE, kv_here * HEAD_SIZE, 1
    )
    basis_folded = jnp.dot(expand_here, compress[0], preferred_element_type=jnp.float32)
    out_folded = jnp.dot(w_out[0], compress[0], preferred_element_type=jnp.float32).astype(
        jnp.bfloat16
    )
    table_rows = embed_table.shape[0]
    local_ids = token_ids.reshape(-1) - lax.axis_index(("segment", "head")) * table_rows
    inside = (local_ids >= 0) & (local_ids < table_rows)
    looked = jnp.take(embed_table, jnp.clip(local_ids, 0, table_rows - 1), axis=0).astype(
        jnp.float32
    )
    picked = jnp.where(inside[:, None], looked, 0.0)
    embedded = lax.psum(picked, ("segment", "head")).astype(jnp.bfloat16)
    tick_count = token_ids.shape[0]
    span_rows = token_ids.shape[1]
    embedded = embedded.reshape(tick_count, span_rows, -1)
    share_rows = span_rows // lax.axis_size("head")
    share_start = head_index * share_rows
    forward_recv = arriving[0]
    backward_recv = returning[0]
    history = []
    forward_shares = []
    backward_shares = []
    for tick_index in range(tick_count):
        more_ticks = tick_index + 1 < tick_count
        forward_in = jnp.where(segment_index == 0, embedded[tick_index], forward_recv)
        backward_in = jnp.where(segment_index == last_segment, seed_grad[tick_index], backward_recv)
        history.append(forward_in)
        delay_ticks = 2 * (last_segment - segment_index)
        replay = stashed[0, tick_index]
        for earlier in range(tick_index + 1):
            replay = jnp.where(delay_ticks == tick_index - earlier, history[earlier], replay)
        partial_value = section_forward(
            forward_in, expand_here, gain_here, query_here, key_here, value_here, out_folded
        )
        direct = precise(forward_in.astype(jnp.float32), basis_folded)
        summed = lax.psum_scatter(
            partial_value.astype(jnp.bfloat16), "head", scatter_dimension=0, tiled=True
        ).astype(jnp.float32)
        own_rows = (summed + lax.dynamic_slice_in_dim(direct, share_start, share_rows, 0)).astype(
            jnp.bfloat16
        )
        forward_shares.append(own_rows)
        if more_ticks:
            arrived = passed_along(own_rows, "segment", 1)
            forward_recv = lax.all_gather(arrived, "head", axis=0, tiled=True)
        partial_back = section_backward(
            replay,
            backward_in,
            expand_here,
            gain_here,
            query_here,
            key_here,
            value_here,
            out_folded,
        )
        direct_back = precise_back(backward_in.astype(jnp.float32), basis_folded)
        summed_back = lax.psum_scatter(
            partial_back.astype(jnp.bfloat16), "head", scatter_dimension=0, tiled=True
        ).astype(jnp.float32)
        own_back = (
            summed_back + lax.dynamic_slice_in_dim(direct_back, share_start, share_rows, 0)
        ).astype(jnp.bfloat16)
        backward_shares.append(own_back)
        if more_ticks:
            arrived_back = passed_along(own_back, "segment", -1)
            backward_recv = lax.all_gather(arrived_back, "head", axis=0, tiled=True)
    sent_forward = jnp.stack(forward_shares)[None]
    sent_backward = jnp.stack(backward_shares)[None]
    return (sent_forward, sent_backward)


def solution(mesh):
    return jax.shard_map(
        shards,
        mesh=mesh,
        in_specs=(
            P("groups", None),
            P(("segment", "head"), None),
            P(("groups", "segment"), None, None),
            P(("groups", "segment"), None, None),
            P(("groups", "segment"), None, None, None),
            P("groups", None, None),
            P("segment", None, None),
            P("segment", None, None),
            P("segment", None),
            P("segment", None, "head"),
            P("segment", None, None),
            P("segment", None, None),
            P("segment", "head", None),
        ),
        out_specs=(
            P(("groups", "segment"), None, "head", None),
            P(("groups", "segment"), None, "head", None),
        ),
        check_vma=False,
    )
```

profile of v0, /device:TPU:0, one launch (start us, length us, event | category | flops | bytes accessed | tf_op | source)
XLA Modules:
  0.0 454.7 jit_solution(9600917615611538147)
XLA Ops:
  9.6 4.0 gather_fusion
  15.9 78.0 %all-reduce.1 = bf16[768,256]{1,0:T(8,128)(2,1)} all-reduce(f32[768,256]{1,0:T(8,128)} %convert_select_fusion), channel_id=1, replica_groups=mesh['groups'=2,'segment'=4,'head'=4] {'segment','head'}, use_global_device_ids=true, to_apply=%region_0.1 | all-reduce | flops 196608 | bytes 1179648 | tf_op jit(solution)/shard_map/psum | solution.py:187
  101.1 6.5 %copy.87 = bf16[1024,2048]{1,0:T(8,128)(2,1)} copy(bf16[1024,2048]{0,1:T(8,128)(2,1)} %bitcast.659) | data formatting | bytes 8388608 | tf_op jit(solution)/shard_map/dot_general | solution.py:57
  107.6 4.0 multiply_reduce_fusion.17
  115.7 3.7 convolution_convert_fusion.5
  123.4 2.7 multiply_reduce_fusion.5
  129.0 2.3 convolution_convert_fusion.2
  131.3 9.0 %reduce-scatter.7.cloned.1.call-done = bf16[64,256]{1,0:T(8,128)(2,1)} async-done(((bf16[256,256]{1,0:T(8,128)(2,1)}), bf16[64,256]{1,0:T(8,128)(2,1)}) %reduce-scatter.7.cloned.1.call-update) | async-done | bytes 32784 | tf_op jit(solution)/shard_map/reduce_scatter | solution.py:211
  146.1 13.8 %all_gather.12 = bf16[256,256]{1,0:T(8,128)(2,1)S(1)} all-gather(bf16[64,256]{1,0:T(8,128)(2,1)} %collective-permute-done), channel_id=1, replica_groups=mesh['groups'=2,'segment'=4,'head'=4] {'head'}, dimensions={0}, use_global_device_ids=true | all-gather | bytes 163840 | tf_op jit(solution)/shard_map/all_gather | solution.py:220
  167.8 2.3 multiply_reduce_fusion.12
  173.0 2.9 multiply_reduce_fusion.14
  177.1 2.5 fusion.24
  179.6 3.8 convolution_convert_fusion.4
  187.6 3.1 fusion.141
  192.2 12.4 %reduce-scatter.9.cloned.1.call-done = bf16[64,256]{1,0:T(8,128)(2,1)} async-done(((bf16[256,256]{1,0:T(8,128)(2,1)}), bf16[64,256]{1,0:T(8,128)(2,1)}) %reduce-scatter.9.cloned.1.call-update) | async-done | bytes 32784 | tf_op jit(solution)/shard_map/reduce_scatter | solution.py:211
  208.6 13.7 %all_gather.13 = bf16[256,256]{1,0:T(8,128)(2,1)S(1)} all-gather(bf16[64,256]{1,0:T(8,128)(2,1)S(1)} %collective-permute-done.1), channel_id=1, replica_groups=mesh['groups'=2,'segment'=4,'head'=4] {'head'}, dimensions={0}, use_global_device_ids=true | all-gather | bytes 163840 | tf_op jit(solution)/shard_map/all_gather | solution.py:220
  227.3 2.3 multiply_reduce_fusion.18
  232.2 3.3 fusion.31
  235.5 5.0 %fusion.19 = (f32[8,256]{1,0:T(8,128)}, f32[256,256,8]{1,0,2:T(8,128)}) fusion(f32[8,256]{1,0:T(8,128)S(1)} %get-tuple-element.5, f32[256,256,8]{1,0,2:T(8,128)} %fusion.141, pred[256,256]{0,1:T(8,128)(4,1)S(1)} %copy-done.28, bf16[256,2048]{1,0:T(8,128)(2,1)} %copy-done.13, bf16[1,2048,512]{2,1,0:T(8,128)(2,1)S(1)} %copy-done, s32[]{:T(128)S(6)} %select_n.142, ...), kind=kOutput, calls=%fused_computation.38 | convolution fusion | flops 271087616 | bytes 6373380 | tf_op jit(solution)/shard_map/iknd,jkd->knij/dot_general | solution.py:110
  240.4 4.1 convert_bitcast_fusion.2
  248.2 2.9 multiply_reduce_fusion.15
  251.1 3.0 copy.65
  257.3 3.6 fusion.4
  260.9 2.9 convolution_add_fusion.5
  263.7 5.1 %multiply_reduce_fusion.4 = (f32[256]{0:T(256)S(1)}, f32[256,2048]{1,0:T(8,128)}) fusion(f32[256,2048]{1,0:T(8,128)} %get-tuple-element.49, f32[2048]{0:T(1024)S(1)} %bitcast.678, f32[256,2048]{1,0:T(8,128)} %convolution_add_fusion.5, bf16[1,2048,512]{2,1,0:T(8,128)(2,1)S(1)} %copy-done, s32[]{:T(128)S(6)} %select_n.142, ...), kind=kOutput, calls=%fused_computation.51 | convolution fusion | flops 270565120 | bytes 8397828 | tf_op jit(solution)/shard_map/dot_general | solution.py:40
  268.8 3.5 convolution_convert_fusion.11
  273.0 3.1 multiply_reduce_fusion.21
  276.1 16.2 %reduce-scatter.13.cloned.1.call-done = bf16[64,256]{1,0:T(8,128)(2,1)} async-done(((bf16[256,256]{1,0:T(8,128)(2,1)}), bf16[64,256]{1,0:T(8,128)(2,1)}) %reduce-scatter.13.cloned.1.call-update) | async-done | bytes 32784 | tf_op jit(solution)/shard_map/reduce_scatter | solution.py:232
  296.2 13.5 %all_gather.14 = bf16[256,256]{1,0:T(8,128)(2,1)S(1)} all-gather(bf16[64,256]{1,0:T(8,128)(2,1)S(1)} %collective-permute-done.2), channel_id=1, replica_groups=mesh['groups'=2,'segment'=4,'head'=4] {'head'}, dimensions={0}, use_global_device_ids=true | all-gather | bytes 163840 | tf_op jit(solution)/shard_map/all_gather | solution.py:241
  312.6 5.0 %fusion.15 = (f32[8,256]{1,0:T(8,128)}, f32[256,256,8]{1,0,2:T(8,128)}) fusion(f32[8,256]{1,0:T(8,128)} %get-tuple-element.6, f32[256,256,8]{1,0,2:T(8,128)} %copy-done.10, pred[256,256]{0,1:T(8,128)(4,1)S(1)} %copy-done.29, bf16[256,2048]{1,0:T(8,128)(2,1)} %copy-done.12, bf16[1,2048,512]{2,1,0:T(8,128)(2,1)S(1)} %copy-done, s32[]{:T(128)S(6)} %select_n.142, ...), kind=kOutput, calls=%fused_computation.32 | convolution fusion | flops 271087616 | bytes 6373380 | tf_op jit(solution)/shard_map/iknd,jkd->knij/dot_general | solution.py:110
  317.6 4.0 convert_bitcast_fusion.1
  326.1 2.6 copy.71
  331.9 3.6 fusion.2
  335.5 2.9 convolution_add_fusion.3
  338.3 5.1 %multiply_reduce_fusion.2 = (f32[256]{0:T(256)S(1)}, f32[256,2048]{1,0:T(8,128)}) fusion(f32[256,2048]{1,0:T(8,128)} %copy-done.3, f32[2048]{0:T(1024)S(1)} %bitcast.679, f32[256,2048]{1,0:T(8,128)} %convolution_add_fusion.3, bf16[1,2048,512]{2,1,0:T(8,128)(2,1)S(1)} %copy-done, s32[]{:T(128)S(6)} %select_n.142, bf16[256,8,128]{2,1,0:T(8,128)(2,1)} %bitcast.671, ...), kind=kOutput, calls=%fused_computation.47 | convolution fusion | flops 270565120 | bytes 8397828 | tf_op jit(solution)/shard_map/dot_general | solution.py:40
  343.4 3.5 convolution_convert_fusion.10
  347.0 3.0 fusion.101
  352.1 12.9 %reduce-scatter.15.cloned.1.call-done = bf16[64,256]{1,0:T(8,128)(2,1)} async-done(((bf16[256,256]{1,0:T(8,128)(2,1)}), bf16[64,256]{1,0:T(8,128)(2,1)}) %reduce-scatter.15.cloned.1.call-update) | async-done | bytes 32784 | tf_op jit(solution)/shard_map/reduce_scatter | solution.py:232
  369.3 13.6 %all_gather.15 = bf16[256,256]{1,0:T(8,128)(2,1)S(1)} all-gather(bf16[64,256]{1,0:T(8,128)(2,1)S(1)} %collective-permute-done.3), channel_id=1, replica_groups=mesh['groups'=2,'segment'=4,'head'=4] {'head'}, dimensions={0}, use_global_device_ids=true | all-gather | bytes 163840 | tf_op jit(solution)/shard_map/all_gather | solution.py:241
  385.8 5.4 %fusion.11 = (f32[8,256]{1,0:T(8,128)S(1)}, f32[8,256]{1,0:T(8,128)S(1)}, f32[256,256,8]{1,0,2:T(8,128)}) fusion(f32[8,256]{1,0:T(8,128)S(1)} %copy-done.68, f32[256,256,8]{1,0,2:T(8,128)} %get-tuple-element.76, pred[256,256]{0,1:T(8,128)(4,1)S(1)} %copy-done.30, f32[256,256,8]{1,0,2:T(8,128)} %fusion.101, bf16[256,2048]{1,0:T(8,128)(2,1)} %copy-done.20, ...), kind=kOutput, calls=%fused_computation.26 | convolution fusion | flops 272658432 | bytes 8478724 | tf_op jit(solution)/shard_map/iknd,jkd->knij/dot_general | solution.py:110
  391.2 4.0 convert_bitcast_fusion
  398.6 3.8 convolution_convert_fusion.3
  402.3 2.7 copy.77
  409.1 3.6 fusion.6
  412.7 2.9 convolution_add_fusion.1
  415.6 5.1 %multiply_reduce_fusion = (f32[256]{0:T(256)S(1)}, f32[256,2048]{1,0:T(8,128)}) fusion(f32[256,2048]{1,0:T(8,128)} %copy-done.2, f32[2048]{0:T(1024)S(1)} %bitcast.680, f32[256,2048]{1,0:T(8,128)} %convolution_add_fusion.1, bf16[1,2048,512]{2,1,0:T(8,128)(2,1)S(1)} %copy-done, s32[]{:T(128)S(6)} %select_n.142, bf16[256,8,128]{2,1,0:T(8,128)(2,1)} %bitcast.670, ...), kind=kOutput, calls=%fused_computation.43 | convolution fusion | flops 270565120 | bytes 8397828 | tf_op jit(solution)/shard_map/dot_general | solution.py:40
  420.7 3.5 convolution_convert_fusion.9
  428.0 17.6 %reduce-scatter.17.cloned.1.call-done = bf16[64,256]{1,0:T(8,128)(2,1)} async-done(((bf16[256,256]{1,0:T(8,128)(2,1)}), bf16[64,256]{1,0:T(8,128)(2,1)}) %reduce-scatter.17.cloned.1.call-update) | async-done | bytes 32784 | tf_op jit(solution)/shard_map/reduce_scatter | solution.py:232
  (266 shorter events, 102.0 us)
Async XLA Ops:
  7.2 108.5 %copy-start = (bf16[1,2048,512]{2,1,0:T(8,128)(2,1)S(1)}, bf16[1,2048,512]{2,1,0:T(8,128)(2,1)}, u32[]{:S(2)}) copy-start(bf16[1,2048,512]{2,1,0:T(8,128)(2,1)} %param.24) | copy-start | bytes 6291460
  7.2 133.1 %reduce-scatter.7.cloned.1.call-start = ((), (), s32[]{:S(2)}) async-start(), calls=%async_computation.6 | async-start | bytes 163840 | tf_op jit(solution)/shard_map/reduce_scatter | solution.py:211
  9.5 106.2 %copy-start.26 = (pred[256,256]{0,1:T(8,128)(4,1)}, pred[256,256]{0,1:T(8,128)(4,1)S(1)}, u32[]{:S(2)}) copy-start(pred[256,256]{0,1:T(8,128)(4,1)S(1)} %iota_compare_fusion) | copy-start | bytes 196612
  9.6 84.3 %copy-start.49 = (bf16[1,256,256]{2,1,0:T(8,128)(2,1)S(1)}, bf16[1,256,256]{2,1,0:T(8,128)(2,1)}, u32[]{:S(2)}) copy-start(bf16[1,256,256]{2,1,0:T(8,128)(2,1)} %param.15) | copy-start | bytes 393220
  13.6 81.3 %copy-start.1 = (bf16[1,256,2048]{2,1,0:T(8,128)(2,1)S(1)}, bf16[1,256,2048]{2,1,0:T(8,128)(2,1)}, u32[]{:S(2)}) copy-start(bf16[1,256,2048]{2,1,0:T(8,128)(2,1)} %param.19) | copy-start | bytes 3145732
  107.6 4.0 copy-start.40
  107.6 4.1 copy-start.77
  121.6 83.0 %reduce-scatter.9.cloned.1.call-start = ((), (), s32[]{:S(2)}) async-start(), calls=%async_computation.7 | async-start | bytes 163840 | tf_op jit(solution)/shard_map/reduce_scatter | solution.py:211
  141.8 4.4 collective-permute-start
  144.2 19.5 %copy-start.66 = (f32[256]{0:T(256)}, f32[256]{0:T(256)S(1)}, u32[]{:S(2)}) copy-start(f32[256]{0:T(256)S(1)} %get-tuple-element.33) | copy-start | bytes 3076
  163.7 4.1 copy-start.15
  164.4 5.7 %copy-start.12 = (bf16[256,2048]{1,0:T(8,128)(2,1)}, bf16[256,2048]{1,0:T(8,128)(2,1)S(1)}, u32[]{:S(2)}) copy-start(bf16[256,2048]{1,0:T(8,128)(2,1)S(1)} %get-tuple-element.19) | copy-start | bytes 3145732
  164.4 6.2 %copy-start.14 = (bf16[256,2048]{1,0:T(8,128)(2,1)}, bf16[256,2048]{1,0:T(8,128)(2,1)S(1)}, u32[]{:S(2)}) copy-start(bf16[256,2048]{1,0:T(8,128)(2,1)S(1)} %get-tuple-element.20) | copy-start | bytes 3145732
  164.4 8.6 %copy-start.13 = (bf16[256,2048]{1,0:T(8,128)(2,1)}, bf16[256,2048]{1,0:T(8,128)(2,1)S(1)}, u32[]{:S(2)}) copy-start(bf16[256,2048]{1,0:T(8,128)(2,1)S(1)} %get-tuple-element.21) | copy-start | bytes 3145732
  173.0 4.1 copy-start.27
  185.6 106.6 %reduce-scatter.13.cloned.1.call-start = ((), (), s32[]{:S(2)}) async-start(), calls=%async_computation.9 | async-start | bytes 163840 | tf_op jit(solution)/shard_map/reduce_scatter | solution.py:232
  185.7 5.0 %copy-start.71 = (f32[256]{0:T(256)S(1)}, f32[256]{0:T(256)}, u32[]{:S(2)}) copy-start(f32[256]{0:T(256)} %get-tuple-element.74) | copy-start | bytes 3076
  185.7 5.6 %copy-start.22 = (bf16[256,256]{1,0:T(8,128)(2,1)S(1)}, bf16[256,256]{1,0:T(8,128)(2,1)}, u32[]{:S(2)}) copy-start(bf16[256,256]{1,0:T(8,128)(2,1)} %copy-done.21) | copy-start | bytes 393220
  205.5 3.1 collective-permute-start.1
  208.5 23.6 %copy-start.10 = (f32[256,256,8]{1,0,2:T(8,128)}, f32[256,256,8]{1,0,2:T(8,128)S(1)}, u32[]{:S(2)}) copy-start(f32[256,256,8]{1,0,2:T(8,128)S(1)} %fusion.142) | copy-start | bytes 6291460
  208.6 15.2 %copy-start.23 = (bf16[256,256]{1,0:T(8,128)(2,1)S(1)}, bf16[256,256]{1,0:T(8,128)(2,1)}, u32[]{:S(2)}) copy-start(bf16[256,256]{1,0:T(8,128)(2,1)} %copy-done.21) | copy-start | bytes 393220
  225.9 3.7 copy-start.16
  230.9 4.5 copy-start.8
  231.5 3.9 copy-start.64
  235.4 5.0 %copy-start.69 = (f32[8,256]{1,0:T(8,128)}, f32[8,256]{1,0:T(8,128)S(1)}, u32[]{:S(2)}) copy-start(f32[8,256]{1,0:T(8,128)S(1)} %get-tuple-element.5) | copy-start | bytes 24580
  240.4 4.1 copy-start.6
  240.4 4.1 copy-start.25
  240.4 4.1 copy-start.48
  263.7 5.1 %copy-start.67 = (f32[256]{0:T(256)S(1)}, f32[256]{0:T(256)}, u32[]{:S(2)}) copy-start(f32[256]{0:T(256)} %copy-done.66) | copy-start | bytes 3076
  263.7 5.1 %copy-start.74 = (f32[256]{0:T(256)S(1)}, f32[256]{0:T(256)}, u32[]{:S(2)}) copy-start(f32[256]{0:T(256)} %get-tuple-element.32) | copy-start | bytes 3076
  272.3 40.3 %copy-start.29 = (pred[256,256]{0,1:T(8,128)(4,1)S(1)}, pred[256,256]{0,1:T(8,128)(4,1)}, u32[]{:S(2)}) copy-start(pred[256,256]{0,1:T(8,128)(4,1)} %copy-done.26) | copy-start | bytes 196612
  272.3 92.7 %reduce-scatter.15.cloned.1.call-start = ((), (), s32[]{:S(2)}) async-start(), calls=%async_computation.10 | async-start | bytes 163840 | tf_op jit(solution)/shard_map/reduce_scatter | solution.py:232
  293.1 24.5 %copy-start.51 = (bf16[64,256]{1,0:T(8,128)(2,1)}, bf16[64,256]{1,0:T(8,128)(2,1)S(1)}, u32[]{:S(2)}) copy-start(bf16[64,256]{1,0:T(8,128)(2,1)S(1)} %add_convert_fusion.2) | copy-start | bytes 98308
  293.1 3.1 collective-permute-start.2
  317.6 4.1 copy-start.5
  317.6 4.1 copy-start.24
  347.0 78.7 %reduce-scatter.11.cloned.1.call-start = ((), (), s32[]{:S(2)}) async-start(), calls=%async_computation.8 | async-start | bytes 163840 | tf_op jit(solution)/shard_map/reduce_scatter | solution.py:211
  350.1 35.7 %copy-start.30 = (pred[256,256]{0,1:T(8,128)(4,1)S(1)}, pred[256,256]{0,1:T(8,128)(4,1)}, u32[]{:S(2)}) copy-start(pred[256,256]{0,1:T(8,128)(4,1)} %copy-done.26) | copy-start | bytes 196612
  350.1 35.7 %copy-start.68 = (f32[8,256]{1,0:T(8,128)S(1)}, f32[8,256]{1,0:T(8,128)}, u32[]{:S(2)}) copy-start(f32[8,256]{1,0:T(8,128)} %get-tuple-element.4) | copy-start | bytes 24580
  365.9 25.3 %copy-start.52 = (bf16[64,256]{1,0:T(8,128)(2,1)}, bf16[64,256]{1,0:T(8,128)(2,1)S(1)}, u32[]{:S(2)}) copy-start(bf16[64,256]{1,0:T(8,128)(2,1)S(1)} %add_convert_fusion.1) | copy-start | bytes 98308
  365.9 3.4 collective-permute-start.3
  391.2 4.0 copy-start.9
  391.2 4.0 copy-start.35
  391.2 4.0 copy-start.54
  402.3 5.0 %copy-start.55 = (f32[256,8]{0,1:T(8,128)S(1)}, f32[256,8]{0,1:T(8,128)}, u32[]{:S(2)}) copy-start(f32[256,8]{0,1:T(8,128)} %get-tuple-element.13) | copy-start | bytes 24580
  407.2 38.3 %reduce-scatter.17.cloned.1.call-start = ((), (), s32[]{:S(2)}) async-start(), calls=%async_computation.11 | async-start | bytes 163840 | tf_op jit(solution)/shard_map/reduce_scatter | solution.py:232
  415.6 5.1 %copy-start.62 = (f32[256]{0:T(256)S(1)}, f32[256]{0:T(256)}, u32[]{:S(2)}) copy-start(f32[256]{0:T(256)} %copy-done.61) | copy-start | bytes 3076
  415.6 5.1 %copy-start.72 = (f32[256]{0:T(256)S(1)}, f32[256]{0:T(256)}, u32[]{:S(2)}) copy-start(f32[256]{0:T(256)} %get-tuple-element.24) | copy-start | bytes 3076
  (40 other events, 99.6 us)
Sparse Core Ops, SparseCore 0:
  121.7 18.5 reduce-scatter.6
  185.7 18.8 reduce-scatter.8
  272.5 19.7 reduce-scatter.12
  347.1 17.8 reduce-scatter.14
  407.3 18.2 reduce-scatter.10
  427.8 17.6 reduce-scatter.16
where the time goes:
time: 463 us; the launch traced here: 455 us
  matrix products  156 us (34%)
  blocking collectives  133 us (29%)
  waiting for transfers between devices  69 us (15%)
  other arithmetic  47.6 us (10%)
  local copies, waits for them, and re-layouts  27.8 us (6%)
  between operations  15.2 us (3%)
  starting transfers between devices  6.18 us (1%)
    psum x1, blocking collectives, shards(): embedded = lax.psum(picked, ('segment', 'head')).astype(jnp.bfloat16)  78 us
    dot_general x15, matrix products, narrow_back(): lax.dot_general(former, latter, (((1,), (1,)), ((), ())), preferred_eleme...  51.8 us
    reduce_scatter x3, waiting for transfers between devices, shards(): lax.psum_scatter(partial_back.astype(jnp.bfloat16), 'head', scatter_dimen...  46.7 us
    all_gather x2, blocking collectives, shards(): forward_recv = lax.all_gather(arrived, 'head', axis=0, tiled=True)  27.6 us
    all_gather x2, blocking collectives, shards(): backward_recv = lax.all_gather(arrived_back, 'head', axis=0, tiled=True)  27.1 us
    reduce_scatter x3, waiting for transfers between devices, shards(): lax.psum_scatter(partial_value.astype(jnp.bfloat16), 'head', scatter_dime...  21.6 us
    dot_general x6, matrix products, probabilities(): jnp.einsum('iknd,jkd->knij', grouped, k_hat, preferred_element_type=jnp.f...  15.6 us
    dot_general x3, matrix products, section_backward(): jnp.einsum('iknd,jkd->knij', grad_attended, values, preferred_element_typ...  15.3 us
  transfers between devices with their start and end apart: 10, of which 7 were waited for; matrix products, arithmetic and copies ran while one was open for 11% of the time, Pallas kernels for 0%

commit v1 on v0

--- a/solution.py
+++ b/solution.py
@@ -184,7 +184,7 @@
         jnp.float32
     )
     picked = jnp.where(inside[:, None], looked, 0.0)
-    embedded = lax.psum(picked, ("segment", "head")).astype(jnp.bfloat16)
+    embedded = jnp.sum(lax.all_gather(picked, ("segment", "head")), axis=0).astype(jnp.bfloat16)
     tick_count = token_ids.shape[0]
     span_rows = token_ids.shape[1]
     embedded = embedded.reshape(tick_count, span_rows, -1)

time: 463 us -> 478 us (1.032)
  waiting for transfers between devices: 69 us -> 163 us
  blocking collectives: 133 us -> 54.5 us
    all_gather x0 -> x1, waiting for transfers between devices: none -> 86.1 us  [shards(): lax.all_gather(picked, ('segment', 'head'))]
    psum x1 -> x0, blocking collectives: 78 us -> none  [shards(): embedded = lax.psum(picked, ('segment', 'head')).astype(jnp.bfloat16)]
    reduce_scatter x3, waiting for transfers between devices: 21.6 us -> 28.8 us  [shards(): lax.psum_scatter(partial_value.astype(jnp.bfloat16), 'head', scatter_dime...]
    reduce_sum x0 -> x1, other arithmetic: none -> 6.27 us  [shards(): jnp.sum(lax.all_gather(picked, ('segment', 'head')), axis=0)]
  transfers between devices with their start and end apart: 10 -> 11, of which waited for: 7 -> 9; matrix products, arithmetic and copies ran while one was open for 11% -> 13% of each run, Pallas kernels for 0% -> 0%
where the time goes in v1:
time: 478 us; the launch traced here: 469 us
  waiting for transfers between devices  163 us (34%)
  matrix products  154 us (32%)
  blocking collectives  54.5 us (11%)
  other arithmetic  51.3 us (11%)
  local copies, waits for them, and re-layouts  25.4 us (5%)
  between operations  15.2 us (3%)
  starting transfers between devices  5.63 us (1%)
    all_gather x1, waiting for transfers between devices, shards(): lax.all_gather(picked, ('segment', 'head'))  86.1 us
    dot_general x15, matrix products, narrow_back(): lax.dot_general(former, latter, (((1,), (1,)), ((), ())), preferred_eleme...  50.9 us
    reduce_scatter x3, waiting for transfers between devices, shards(): lax.psum_scatter(partial_back.astype(jnp.bfloat16), 'head', scatter_dimen...  46.8 us
    reduce_scatter x3, waiting for transfers between devices, shards(): lax.psum_scatter(partial_value.astype(jnp.bfloat16), 'head', scatter_dime...  28.8 us
    all_gather x2, blocking collectives, shards(): forward_recv = lax.all_gather(arrived, 'head', axis=0, tiled=True)  27.4 us
    all_gather x2, blocking collectives, shards(): backward_recv = lax.all_gather(arrived_back, 'head', axis=0, tiled=True)  27.1 us
    dot_general x6, matrix products, probabilities(): jnp.einsum('iknd,jkd->knij', grouped, k_hat, preferred_element_type=jnp.f...  15.5 us
    dot_general x3, matrix products, section_backward(): jnp.einsum('iknd,jkd->knij', grad_attended, values, preferred_element_typ...  15.4 us
  transfers between devices with their start and end apart: 11, of which 9 were waited for; matrix products, arithmetic and copies ran while one was open for 13% of the time, Pallas kernels for 0%

profile of v1, /device:TPU:0, one launch (start us, length us, event | category | flops | bytes accessed | tf_op | source)
XLA Modules:
  0.0 468.7 jit_solution(1691144233359509745)
XLA Ops:
  9.5 3.2 gather_fusion
  14.1 3.8 fusion.32
  20.2 6.7 %copy.123 = bf16[1024,2048]{1,0:T(8,128)(2,1)} copy(bf16[1024,2048]{0,1:T(8,128)(2,1)} %bitcast.663) | data formatting | bytes 8388608 | tf_op jit(solution)/shard_map/dot_general | solution.py:57
  31.2 86.1 %all-gather.2.cloned.1.call-done = f32[16,768,256]{2,1,0:T(8,128)} async-done(((f32[1,768,256]{2,1,0:T(8,128)}), f32[16,768,256]{2,1,0:T(8,128)}) %all-gather.2.cloned.1.call-update) | async-done | bytes 12582928 | tf_op jit(solution)/shard_map/all_gather | solution.py:187
  117.3 6.3 %reduce_sum.357 = bf16[768,256]{1,0:T(8,128)(2,1)} reduce(f32[16,768,256]{2,1,0:T(8,128)} %all-gather.2.cloned.1.call-done, f32[]{:T(128)} %constant.94.clone.1), dimensions={0}, to_apply=%region_0.1 | reduce | flops 2949120 | bytes 12976132 | tf_op jit(solution)/shard_map/reduce_sum | solution.py:187
  131.1 3.7 convolution_convert_fusion.5
  137.0 2.7 multiply_reduce_fusion.5
  140.8 14.1 %reduce-scatter.7.cloned.1.call-done = bf16[64,256]{1,0:T(8,128)(2,1)} async-done(((bf16[256,256]{1,0:T(8,128)(2,1)}), bf16[64,256]{1,0:T(8,128)(2,1)}) %reduce-scatter.7.cloned.1.call-update) | async-done | bytes 32784 | tf_op jit(solution)/shard_map/reduce_scatter | solution.py:211
  157.9 13.6 %all_gather.17 = bf16[256,256]{1,0:T(8,128)(2,1)S(1)} all-gather(bf16[64,256]{1,0:T(8,128)(2,1)S(1)} %collective-permute-done), channel_id=1, replica_groups=mesh['groups'=2,'segment'=4,'head'=4] {'head'}, dimensions={0}, use_global_device_ids=true | all-gather | bytes 163840 | tf_op jit(solution)/shard_map/all_gather | solution.py:220
  179.3 2.3 multiply_reduce_fusion.12
  184.5 2.9 multiply_reduce_fusion.14
  188.6 2.5 fusion.24
  191.1 3.7 convolution_convert_fusion.4
  199.1 3.1 fusion.141
  203.8 14.5 %reduce-scatter.9.cloned.1.call-done = bf16[64,256]{1,0:T(8,128)(2,1)} async-done(((bf16[256,256]{1,0:T(8,128)(2,1)}), bf16[64,256]{1,0:T(8,128)(2,1)}) %reduce-scatter.9.cloned.1.call-update) | async-done | bytes 32784 | tf_op jit(solution)/shard_map/reduce_scatter | solution.py:211
  222.2 13.8 %all_gather.18 = bf16[256,256]{1,0:T(8,128)(2,1)S(1)} all-gather(bf16[64,256]{1,0:T(8,128)(2,1)S(1)} %collective-permute-done.1), channel_id=1, replica_groups=mesh['groups'=2,'segment'=4,'head'=4] {'head'}, dimensions={0}, use_global_device_ids=true | all-gather | bytes 163840 | tf_op jit(solution)/shard_map/all_gather | solution.py:220
  240.9 2.3 multiply_reduce_fusion.18
  245.8 3.2 fusion.31
  249.1 5.0 %fusion.19 = (f32[8,256]{1,0:T(8,128)}, f32[256,256,8]{1,0,2:T(8,128)}) fusion(f32[8,256]{1,0:T(8,128)S(1)} %get-tuple-element.5, f32[256,256,8]{1,0,2:T(8,128)} %fusion.141, pred[256,256]{0,1:T(8,128)(4,1)S(1)} %copy-done.30, bf16[256,2048]{1,0:T(8,128)(2,1)} %copy-done.14, bf16[1,2048,512]{2,1,0:T(8,128)(2,1)S(1)} %copy-done, s32[]{:T(128)S(6)} %select_n.156, ...), kind=kOutput, calls=%fused_computation.38 | convolution fusion | flops 271087616 | bytes 6373380 | tf_op jit(solution)/shard_map/iknd,jkd->knij/dot_general | solution.py:110
  254.1 4.1 convert_bitcast_fusion.2
  261.8 2.9 multiply_reduce_fusion.15
  264.7 3.0 copy.101
  270.9 3.6 fusion.4
  274.5 2.9 convolution_add_fusion.5
  277.4 5.1 %multiply_reduce_fusion.4 = (f32[256]{0:T(256)S(1)}, f32[256,2048]{1,0:T(8,128)}) fusion(f32[256,2048]{1,0:T(8,128)} %get-tuple-element.49, f32[2048]{0:T(1024)S(1)} %bitcast.682, f32[256,2048]{1,0:T(8,128)} %convolution_add_fusion.5, bf16[1,2048,512]{2,1,0:T(8,128)(2,1)S(1)} %copy-done, s32[]{:T(128)S(6)} %select_n.156, ...), kind=kOutput, calls=%fused_computation.51 | convolution fusion | flops 270565120 | bytes 8397828 | tf_op jit(solution)/shard_map/dot_general | solution.py:40
  282.5 3.5 convolution_convert_fusion.11
  286.6 3.0 multiply_reduce_fusion.21
  289.7 16.3 %reduce-scatter.13.cloned.1.call-done = bf16[64,256]{1,0:T(8,128)(2,1)} async-done(((bf16[256,256]{1,0:T(8,128)(2,1)}), bf16[64,256]{1,0:T(8,128)(2,1)}) %reduce-scatter.13.cloned.1.call-update) | async-done | bytes 32784 | tf_op jit(solution)/shard_map/reduce_scatter | solution.py:232
  309.9 13.5 %all_gather.19 = bf16[256,256]{1,0:T(8,128)(2,1)S(1)} all-gather(bf16[64,256]{1,0:T(8,128)(2,1)S(1)} %collective-permute-done.2), channel_id=1, replica_groups=mesh['groups'=2,'segment'=4,'head'=4] {'head'}, dimensions={0}, use_global_device_ids=true | all-gather | bytes 163840 | tf_op jit(solution)/shard_map/all_gather | solution.py:241
  326.4 5.0 %fusion.15 = (f32[8,256]{1,0:T(8,128)}, f32[256,256,8]{1,0,2:T(8,128)}) fusion(f32[8,256]{1,0:T(8,128)} %get-tuple-element.6, f32[256,256,8]{1,0,2:T(8,128)} %copy-done.10, pred[256,256]{0,1:T(8,128)(4,1)S(1)} %copy-done.31, bf16[256,2048]{1,0:T(8,128)(2,1)} %copy-done.13, bf16[1,2048,512]{2,1,0:T(8,128)(2,1)S(1)} %copy-done, s32[]{:T(128)S(6)} %select_n.156, ...), kind=kOutput, calls=%fused_computation.32 | convolution fusion | flops 271087616 | bytes 6373380 | tf_op jit(solution)/shard_map/iknd,jkd->knij/dot_general | solution.py:110
  331.4 4.0 convert_bitcast_fusion.1
  339.9 2.7 copy.107
  345.7 3.6 fusion.2
  349.3 2.9 convolution_add_fusion.3
  352.2 5.1 %multiply_reduce_fusion.2 = (f32[256]{0:T(256)S(1)}, f32[256,2048]{1,0:T(8,128)}) fusion(f32[256,2048]{1,0:T(8,128)} %copy-done.3, f32[2048]{0:T(1024)S(1)} %bitcast.683, f32[256,2048]{1,0:T(8,128)} %convolution_add_fusion.3, bf16[1,2048,512]{2,1,0:T(8,128)(2,1)S(1)} %copy-done, s32[]{:T(128)S(6)} %select_n.156, bf16[256,8,128]{2,1,0:T(8,128)(2,1)} %bitcast.675, ...), kind=kOutput, calls=%fused_computation.47 | convolution fusion | flops 270565120 | bytes 8397828 | tf_op jit(solution)/shard_map/dot_general | solution.py:40
  357.3 3.5 convolution_convert_fusion.10
  360.9 3.0 fusion.101
  366.0 12.9 %reduce-scatter.15.cloned.1.call-done = bf16[64,256]{1,0:T(8,128)(2,1)} async-done(((bf16[256,256]{1,0:T(8,128)(2,1)}), bf16[64,256]{1,0:T(8,128)(2,1)}) %reduce-scatter.15.cloned.1.call-update) | async-done | bytes 32784 | tf_op jit(solution)/shard_map/reduce_scatter | solution.py:232
  383.1 13.6 %all_gather.20 = bf16[256,256]{1,0:T(8,128)(2,1)S(1)} all-gather(bf16[64,256]{1,0:T(8,128)(2,1)S(1)} %collective-permute-done.3), channel_id=1, replica_groups=mesh['groups'=2,'segment'=4,'head'=4] {'head'}, dimensions={0}, use_global_device_ids=true | all-gather | bytes 163840 | tf_op jit(solution)/shard_map/all_gather | solution.py:241
  399.6 5.4 %fusion.11 = (f32[8,256]{1,0:T(8,128)S(1)}, f32[8,256]{1,0:T(8,128)S(1)}, f32[256,256,8]{1,0,2:T(8,128)}) fusion(f32[8,256]{1,0:T(8,128)S(1)} %copy-done.70, f32[256,256,8]{1,0,2:T(8,128)} %get-tuple-element.76, pred[256,256]{0,1:T(8,128)(4,1)S(1)} %copy-done.32, f32[256,256,8]{1,0,2:T(8,128)} %fusion.101, bf16[256,2048]{1,0:T(8,128)(2,1)} %copy-done.22, ...), kind=kOutput, calls=%fused_computation.26 | convolution fusion | flops 272658432 | bytes 8478724 | tf_op jit(solution)/shard_map/iknd,jkd->knij/dot_general | solution.py:110
  405.1 4.1 convert_bitcast_fusion
  412.5 3.7 convolution_convert_fusion.3
  416.3 2.7 copy.113
  423.0 3.6 fusion.6
  426.6 2.8 convolution_add_fusion.1
  429.5 5.1 %multiply_reduce_fusion = (f32[256]{0:T(256)S(1)}, f32[256,2048]{1,0:T(8,128)}) fusion(f32[256,2048]{1,0:T(8,128)} %copy-done.2, f32[2048]{0:T(1024)S(1)} %bitcast.684, f32[256,2048]{1,0:T(8,128)} %convolution_add_fusion.1, bf16[1,2048,512]{2,1,0:T(8,128)(2,1)S(1)} %copy-done, s32[]{:T(128)S(6)} %select_n.156, bf16[256,8,128]{2,1,0:T(8,128)(2,1)} %bitcast.674, ...), kind=kOutput, calls=%fused_computation.43 | convolution fusion | flops 270565120 | bytes 8397828 | tf_op jit(solution)/shard_map/dot_general | solution.py:40
  434.6 3.5 convolution_convert_fusion.9
  441.9 17.6 %reduce-scatter.17.cloned.1.call-done = bf16[64,256]{1,0:T(8,128)(2,1)} async-done(((bf16[256,256]{1,0:T(8,128)(2,1)}), bf16[64,256]{1,0:T(8,128)(2,1)}) %reduce-scatter.17.cloned.1.call-update) | async-done | bytes 32784 | tf_op jit(solution)/shard_map/reduce_scatter | solution.py:232
  (271 shorter events, 97.3 us)
Async XLA Ops:
  7.2 123.9 %copy-start = (bf16[1,2048,512]{2,1,0:T(8,128)(2,1)S(1)}, bf16[1,2048,512]{2,1,0:T(8,128)(2,1)}, u32[]{:S(2)}) copy-start(bf16[1,2048,512]{2,1,0:T(8,128)(2,1)} %param.24) | copy-start | bytes 6291460
  7.2 110.1 %all-gather.2.cloned.1.call-start = ((), (), s32[]{:S(2)}) async-start(), calls=%async_computation.6 | async-start | bytes 13369344 | tf_op jit(solution)/shard_map/all_gather | solution.py:187
  14.0 140.9 %reduce-scatter.7.cloned.1.call-start = ((), (), s32[]{:S(2)}) async-start(), calls=%async_computation.7 | async-start | bytes 163840 | tf_op jit(solution)/shard_map/reduce_scatter | solution.py:211
  14.1 3.8 copy-start.46
  20.2 7.3 %copy-start.1 = (bf16[1,256,2048]{2,1,0:T(8,128)(2,1)S(1)}, bf16[1,256,2048]{2,1,0:T(8,128)(2,1)}, u32[]{:S(2)}) copy-start(bf16[1,256,2048]{2,1,0:T(8,128)(2,1)} %param.19) | copy-start | bytes 3145732
  125.4 3.8 copy-start.20
  137.0 81.2 %reduce-scatter.9.cloned.1.call-start = ((), (), s32[]{:S(2)}) async-start(), calls=%async_computation.8 | async-start | bytes 163840 | tf_op jit(solution)/shard_map/reduce_scatter | solution.py:211
  155.7 2.1 collective-permute-start
  157.6 17.6 %copy-start.68 = (f32[256]{0:T(256)}, f32[256]{0:T(256)S(1)}, u32[]{:S(2)}) copy-start(f32[256]{0:T(256)S(1)} %get-tuple-element.33) | copy-start | bytes 3076
  175.2 4.1 copy-start.17
  175.9 5.7 %copy-start.13 = (bf16[256,2048]{1,0:T(8,128)(2,1)}, bf16[256,2048]{1,0:T(8,128)(2,1)S(1)}, u32[]{:S(2)}) copy-start(bf16[256,2048]{1,0:T(8,128)(2,1)S(1)} %get-tuple-element.19) | copy-start | bytes 3145732
  175.9 6.2 %copy-start.15 = (bf16[256,2048]{1,0:T(8,128)(2,1)}, bf16[256,2048]{1,0:T(8,128)(2,1)S(1)}, u32[]{:S(2)}) copy-start(bf16[256,2048]{1,0:T(8,128)(2,1)S(1)} %get-tuple-element.20) | copy-start | bytes 3145732
  175.9 8.6 %copy-start.14 = (bf16[256,2048]{1,0:T(8,128)(2,1)}, bf16[256,2048]{1,0:T(8,128)(2,1)S(1)}, u32[]{:S(2)}) copy-start(bf16[256,2048]{1,0:T(8,128)(2,1)S(1)} %get-tuple-element.21) | copy-start | bytes 3145732
  184.5 4.1 copy-start.29
  197.1 108.9 %reduce-scatter.13.cloned.1.call-start = ((), (), s32[]{:S(2)}) async-start(), calls=%async_computation.10 | async-start | bytes 163840 | tf_op jit(solution)/shard_map/reduce_scatter | solution.py:232
  197.1 5.1 %copy-start.73 = (f32[256]{0:T(256)S(1)}, f32[256]{0:T(256)}, u32[]{:S(2)}) copy-start(f32[256]{0:T(256)} %get-tuple-element.74) | copy-start | bytes 3076
  197.1 5.6 %copy-start.24 = (bf16[256,256]{1,0:T(8,128)(2,1)S(1)}, bf16[256,256]{1,0:T(8,128)(2,1)}, u32[]{:S(2)}) copy-start(bf16[256,256]{1,0:T(8,128)(2,1)} %copy-done.23) | copy-start | bytes 393220
  219.1 3.1 collective-permute-start.1
  222.2 23.6 %copy-start.10 = (f32[256,256,8]{1,0,2:T(8,128)}, f32[256,256,8]{1,0,2:T(8,128)S(1)}, u32[]{:S(2)}) copy-start(f32[256,256,8]{1,0,2:T(8,128)S(1)} %fusion.142) | copy-start | bytes 6291460
  222.2 15.3 %copy-start.25 = (bf16[256,256]{1,0:T(8,128)(2,1)S(1)}, bf16[256,256]{1,0:T(8,128)(2,1)}, u32[]{:S(2)}) copy-start(bf16[256,256]{1,0:T(8,128)(2,1)} %copy-done.23) | copy-start | bytes 393220
  239.5 3.7 copy-start.18
  240.9 3.6 copy-start.22
  244.6 4.5 copy-start.8
  245.2 3.9 copy-start.66
  249.0 5.0 %copy-start.71 = (f32[8,256]{1,0:T(8,128)}, f32[8,256]{1,0:T(8,128)S(1)}, u32[]{:S(2)}) copy-start(f32[8,256]{1,0:T(8,128)S(1)} %get-tuple-element.5) | copy-start | bytes 24580
  254.0 4.1 copy-start.6
  254.0 4.1 copy-start.27
  254.0 4.1 copy-start.50
  277.4 5.1 %copy-start.69 = (f32[256]{0:T(256)S(1)}, f32[256]{0:T(256)}, u32[]{:S(2)}) copy-start(f32[256]{0:T(256)} %copy-done.68) | copy-start | bytes 3076
  277.4 5.1 %copy-start.76 = (f32[256]{0:T(256)S(1)}, f32[256]{0:T(256)}, u32[]{:S(2)}) copy-start(f32[256]{0:T(256)} %get-tuple-element.32) | copy-start | bytes 3076
  286.0 40.4 %copy-start.31 = (pred[256,256]{0,1:T(8,128)(4,1)S(1)}, pred[256,256]{0,1:T(8,128)(4,1)}, u32[]{:S(2)}) copy-start(pred[256,256]{0,1:T(8,128)(4,1)} %iota_compare_fusion) | copy-start | bytes 196612
  286.0 92.9 %reduce-scatter.15.cloned.1.call-start = ((), (), s32[]{:S(2)}) async-start(), calls=%async_computation.11 | async-start | bytes 163840 | tf_op jit(solution)/shard_map/reduce_scatter | solution.py:232
  306.8 24.5 %copy-start.53 = (bf16[64,256]{1,0:T(8,128)(2,1)}, bf16[64,256]{1,0:T(8,128)(2,1)S(1)}, u32[]{:S(2)}) copy-start(bf16[64,256]{1,0:T(8,128)(2,1)S(1)} %add_convert_fusion.2) | copy-start | bytes 98308
  306.8 3.1 collective-permute-start.2
  331.4 4.0 copy-start.5
  331.4 4.0 copy-start.26
  360.9 78.7 %reduce-scatter.11.cloned.1.call-start = ((), (), s32[]{:S(2)}) async-start(), calls=%async_computation.9 | async-start | bytes 163840 | tf_op jit(solution)/shard_map/reduce_scatter | solution.py:211
  363.9 35.7 %copy-start.32 = (pred[256,256]{0,1:T(8,128)(4,1)S(1)}, pred[256,256]{0,1:T(8,128)(4,1)}, u32[]{:S(2)}) copy-start(pred[256,256]{0,1:T(8,128)(4,1)} %iota_compare_fusion) | copy-start | bytes 196612
  363.9 35.7 %copy-start.70 = (f32[8,256]{1,0:T(8,128)S(1)}, f32[8,256]{1,0:T(8,128)}, u32[]{:S(2)}) copy-start(f32[8,256]{1,0:T(8,128)} %get-tuple-element.4) | copy-start | bytes 24580
  379.7 25.3 %copy-start.54 = (bf16[64,256]{1,0:T(8,128)(2,1)}, bf16[64,256]{1,0:T(8,128)(2,1)S(1)}, u32[]{:S(2)}) copy-start(bf16[64,256]{1,0:T(8,128)(2,1)S(1)} %add_convert_fusion.1) | copy-start | bytes 98308
  379.7 3.4 collective-permute-start.3
  405.1 4.1 copy-start.9
  405.1 4.1 copy-start.38
  405.1 4.1 copy-start.56
  416.3 5.0 %copy-start.57 = (f32[256,8]{0,1:T(8,128)S(1)}, f32[256,8]{0,1:T(8,128)}, u32[]{:S(2)}) copy-start(f32[256,8]{0,1:T(8,128)} %get-tuple-element.13) | copy-start | bytes 24580
  421.1 38.4 %reduce-scatter.17.cloned.1.call-start = ((), (), s32[]{:S(2)}) async-start(), calls=%async_computation.12 | async-start | bytes 163840 | tf_op jit(solution)/shard_map/reduce_scatter | solution.py:232
  429.5 5.1 %copy-start.64 = (f32[256]{0:T(256)S(1)}, f32[256]{0:T(256)}, u32[]{:S(2)}) copy-start(f32[256]{0:T(256)} %copy-done.63) | copy-start | bytes 3076
  429.5 5.1 %copy-start.74 = (f32[256]{0:T(256)S(1)}, f32[256]{0:T(256)}, u32[]{:S(2)}) copy-start(f32[256]{0:T(256)} %get-tuple-element.24) | copy-start | bytes 3076
  (42 other events, 100.2 us)
Sparse Core Ops, SparseCore 0:
  14.1 103.1 all-gather.1
  137.1 17.6 reduce-scatter.6
  197.2 20.9 reduce-scatter.8
  286.1 19.8 reduce-scatter.12
  361.0 17.8 reduce-scatter.14
  421.3 18.2 reduce-scatter.10
  441.8 17.6 reduce-scatter.16
